TPU v7x, 32 devices: a whole 2x2x4 slice. The times are simulated.
32 devices in a mesh: dp: 8 (over z, y), mp: 4 (over x, core).
Axes of the slice: x: 2, y: 2, z: 4, core: 2. Of those that a mesh axis runs over, the one named last changes fastest.
Arguments:
- tokens: bfloat16 [16, 1024, 1024], P(None, ('dp', 'mp')), may hold values from -6 to 6
- encoder: bfloat16 [16, 1024, 1024], P(None, ('dp', 'mp')), may hold values from -6 to 6
- cotangent: bfloat16 [16, 1024, 1024], P(None, ('dp', 'mp')), may hold values from -6 to 6
- lengths: int32 [16], replicated, may hold values from 1 to 1024, 8192 in all
- deal: int32 [16], replicated, may hold values from 0 to 15, each once
- attn_in: float32 [6, 1024, 1024], P(None, 'dp', 'mp'), may hold values from -0.16 to 0.16
- attn_out: float32 [2, 1024, 1024], P(None, 'mp', 'dp'), may hold values from -0.75 to 0.75
- ff_in: float32 [2, 1024, 2816], P(None, 'dp', 'mp'), may hold values from -0.1875 to 0.1875
- ff_out: float32 [2816, 1024], P('mp', 'dp'), may hold values from -0.109375 to 0.109375
- gains: float32 [3, 1024], P(None, 'dp'), may hold values from 0.5 to 1.5
- mom_attn_in: float32 [6, 1024, 1024], P(None, 'dp', 'mp'), may hold values from -6 to 6
- mom_attn_out: float32 [2, 1024, 1024], P(None, 'mp', 'dp'), may hold values from -6 to 6
- mom_ff_in: float32 [2, 1024, 2816], P(None, 'dp', 'mp'), may hold values from -6 to 6
- mom_ff_out: float32 [2816, 1024], P('mp', 'dp'), may hold values from -6 to 6
- mom_gains: float32 [3, 1024], P(None, 'dp'), may hold values from -6 to 6
- avg_attn_in: float32 [6, 1024, 1024], P(None, 'dp', 'mp'), may hold values from -0.1875 to 0.1875
- avg_attn_out: float32 [2, 1024, 1024], P(None, 'mp', 'dp'), may hold values from -0.75 to 0.75
- avg_ff_in: float32 [2, 1024, 2816], P(None, 'dp', 'mp'), may hold values from -0.1875 to 0.1875
- avg_ff_out: float32 [2816, 1024], P('mp', 'dp'), may hold values from -0.109375 to 0.109375
- avg_gains: float32 [3, 1024], P(None, 'dp'), may hold values from 0.5 to 1.5
Outputs:
- block_output: float32 [16, 1024, 1024], P(None, ('dp', 'mp'))
- grad_tokens: float32 [16, 1024, 1024], P(None, ('dp', 'mp'))
- grad_encoder: float32 [16, 1024, 1024], P(None, ('dp', 'mp'))
- grad_attn_in: float32 [6, 1024, 1024], P(None, 'dp', 'mp')
- moment_attn_in: float32 [6, 1024, 1024], P(None, 'dp', 'mp')
- average_attn_in: float32 [6, 1024, 1024], P(None, 'dp', 'mp')
- master_attn_in: float32 [6, 1024, 1024], P(None, 'dp', 'mp')
- grad_attn_out: float32 [2, 1024, 1024], P(None, 'mp', 'dp')
- moment_attn_out: float32 [2, 1024, 1024], P(None, 'mp', 'dp')
- average_attn_out: float32 [2, 1024, 1024], P(None, 'mp', 'dp')
- master_attn_out: float32 [2, 1024, 1024], P(None, 'mp', 'dp')
- grad_ff_in: float32 [2, 1024, 2816], P(None, 'dp', 'mp')
- moment_ff_in: float32 [2, 1024, 2816], P(None, 'dp', 'mp')
- average_ff_in: float32 [2, 1024, 2816], P(None, 'dp', 'mp')
- master_ff_in: float32 [2, 1024, 2816], P(None, 'dp', 'mp')
- grad_ff_out: float32 [2816, 1024], P('mp', 'dp')
- moment_ff_out: float32 [2816, 1024], P('mp', 'dp')
- average_ff_out: float32 [2816, 1024], P('mp', 'dp')
- master_ff_out: float32 [2816, 1024], P('mp', 'dp')
- grad_gains: float32 [3, 1024], P(None, 'dp')
- moment_gains: float32 [3, 1024], P(None, 'dp')
- average_gains: float32 [3, 1024], P(None, 'dp')
- master_gains: float32 [3, 1024], P(None, 'dp')
- head_maxima: float32 [16], P('mp')
- clip_factors: float32 [16], P('mp')
Inputs may be any that keep to these rules, and one draw needn't show every extreme that they name: lengths[j] counts the real tokens of slot j; positions from lengths[j] on are padding. deal holds each slot once; slot j is micro-batch j % 2 of data index j // 2.
All inputs are finite; a program needn't handle non-finite values.
Results may differ from a plain program's by a relative error of at most 0.025.
The roundings to bfloat16 on the way count: a program that leaves them out, or rounds other values in their place, can miss the bound.
Values may be sent and summed in bfloat16 or wider, within the bound.
No kernel may reach another device: no remote copies, remote signals or barrier semaphores. Data moves between devices by JAX's collectives and lax.ppermute only.
A program may use at most 256 MiB of HBM per device.

v0:
```python
import jax
import jax.numpy as jnp
from jax import lax
from jax.sharding import Mesh, PartitionSpec as P

D = 1024
DK = 64
epsilon = 1e-06
clip_limit = 10.0
momentum_rate = 0.9
learn_rate = 0.01
average_rate = 0.5
neg_large = -1e30
bf16 = jnp.bfloat16
f32 = jnp.float32
swap = ((0, 1), (1, 0))
chips = ("dp", "mx")


def rms_norm(hidden, gain_vec):
    row_scale = lax.rsqrt(jnp.mean(hidden * hidden, axis=-1, keepdims=True) + epsilon)
    return hidden * row_scale * gain_vec


def gelu_product(gate_part, up_part):
    return jax.nn.gelu(gate_part, approximate=True) * up_part


def nn(left, right):
    return lax.dot_general(left, right, (((1,), (0,)), ((), ())), preferred_element_type=f32)


def nt(left, right):
    return lax.dot_general(left, right, (((1,), (1,)), ((), ())), preferred_element_type=f32)


def tn(left, right):
    return lax.dot_general(left, right, (((0,), (0,)), ((), ())), preferred_element_type=f32)


def both_cores(own):
    return jnp.concatenate([own, lax.ppermute(own, "mc", swap)], axis=0)


def sum_cores(parts):
    own, other = parts
    return own + lax.ppermute(other, "mc", swap)


def split_heads(values):
    return values.reshape(values.shape[0], values.shape[1] // DK, DK)


def attend(query, keys, values, allowed):
    query_h, keys_h, values_h = (split_heads(query), split_heads(keys), split_heads(values))
    scores = jnp.einsum("qhe,khe->hqk", query_h, keys_h, preferred_element_type=f32)
    masked = jnp.where(allowed, scores, neg_large)
    row_top = jnp.max(masked, axis=-1, keepdims=True)
    expo_rows = jnp.exp(masked - row_top)
    row_total = jnp.sum(expo_rows, axis=-1, keepdims=True)
    soft_rows = expo_rows / row_total
    mixed = jnp.einsum("hqk,khe->qhe", soft_rows.astype(bf16), values_h, preferred_element_type=f32)
    return (mixed.reshape(query.shape).astype(bf16), row_top + jnp.log(row_total), row_top)


def attend_back(query, keys, values, allowed, log_total, grad_mixed):
    query_h, keys_h, values_h = (split_heads(query), split_heads(keys), split_heads(values))
    grad_h = split_heads(grad_mixed)
    scores = jnp.einsum("qhe,khe->hqk", query_h, keys_h, preferred_element_type=f32)
    soft_rows = jnp.exp(jnp.where(allowed, scores, neg_large) - log_total)
    grad_soft = jnp.einsum("qhe,khe->hqk", grad_h, values_h, preferred_element_type=f32)
    grad_values = jnp.einsum(
        "hqk,qhe->khe", soft_rows.astype(bf16), grad_h, preferred_element_type=f32
    )
    row_dot = jnp.sum(grad_soft * soft_rows, axis=-1, keepdims=True)
    grad_scores = (soft_rows * (grad_soft - row_dot)).astype(bf16)
    grad_query = jnp.einsum("hqk,khe->qhe", grad_scores, keys_h, preferred_element_type=f32)
    grad_keys = jnp.einsum("hqk,qhe->khe", grad_scores, query_h, preferred_element_type=f32)
    return tuple(
        (t.reshape(t.shape[0], -1).astype(bf16) for t in (grad_query, grad_keys, grad_values))
    )


def norm_back(hidden, gain_vec, grad):
    row_scale = lax.rsqrt(jnp.mean(hidden * hidden, axis=-1, keepdims=True) + epsilon)
    z = hidden * row_scale
    grad_z = grad * gain_vec
    grad_hidden = row_scale * (grad_z - z * jnp.mean(grad_z * z, axis=-1, keepdims=True))
    return (grad_hidden, jnp.sum(grad * z, axis=0))


def apply_update(weight, grad_sum, moment, average, factor, grad_scale):
    grad_now = grad_sum * grad_scale
    moment_new = momentum_rate * moment + grad_now
    master_new = (weight - learn_rate * (grad_now + momentum_rate * moment_new)) * factor
    average_new = average_rate * average + (1.0 - average_rate) * master_new
    return (grad_now, moment_new, average_new, master_new)


def flat_columns(block):
    return jnp.swapaxes(block, 0, 1).reshape(block.shape[1], -1)


def gather_chunk(local):
    own = lax.all_gather(local, "dp", axis=0, tiled=True)
    return (own, lax.ppermute(own, "mx", swap))


def reduce_chunk(own, other):
    arrived = lax.ppermute(other.astype(bf16), "mx", swap)
    total = (own + arrived.astype(f32)).astype(bf16)
    return lax.psum_scatter(total, "dp", scatter_dimension=0, tiled=True).astype(f32)


def on_device(
    tokens,
    encoder,
    cotangent,
    lengths,
    deal,
    attn_in,
    attn_out,
    ff_in,
    ff_out,
    gains,
    mom_attn_in,
    mom_attn_out,
    mom_ff_in,
    mom_ff_out,
    mom_gains,
    avg_attn_in,
    avg_attn_out,
    avg_ff_in,
    avg_ff_out,
    avg_gains,
):
    seq_count, block_rows = (tokens.shape[0], tokens.shape[1])
    core = lax.axis_index("mc")
    chip = lax.axis_index("dp") * lax.axis_size("mx") + lax.axis_index("mx")
    own_rows = block_rows * seq_count
    slot_len = 2 * own_rows
    heads_cols = attn_in.shape[2]
    hidden = ff_in.shape[2]
    model_rows = attn_in.shape[1]

    def to_chips(values):
        moved = lax.all_to_all(values, chips, split_axis=0, concat_axis=1, tiled=True)
        return moved.reshape(own_rows, D)

    def from_chips(rows):
        return lax.all_to_all(
            rows.reshape(1, own_rows, D), chips, split_axis=1, concat_axis=0, tiled=True
        ).astype(f32)

    seq_len = lengths[deal[chip]]
    row_ids = jnp.arange(own_rows, dtype=jnp.int32)
    lane = row_ids % block_rows
    pos_own = (row_ids // block_rows * 2 + core) * block_rows + lane
    pos_other = (row_ids // block_rows * 2 + 1 - core) * block_rows + lane
    pos = jnp.concatenate([pos_own, pos_other])
    allowed = pos[None, :] <= pos[:, None]
    valid_own = (pos_own < seq_len).astype(f32)[:, None]
    valid_all = pos < seq_len
    pad = jnp.zeros((model_rows, 125), bf16)
    chunk_a = jnp.concatenate(
        [flat_columns(attn_in[0:3].astype(bf16)), gains.astype(bf16).T, pad], axis=1
    )
    out_t = jnp.swapaxes(attn_out.astype(bf16), 1, 2)
    chunk_b = jnp.concatenate([out_t[0], flat_columns(attn_in[3:6].astype(bf16)), out_t[1]], axis=1)
    chunk_c = flat_columns(ff_in.astype(bf16))
    chunk_d = ff_out.astype(bf16).T
    tok_own = to_chips(tokens)
    got_a = gather_chunk(chunk_a)
    enc_own = to_chips(encoder)
    got_b = gather_chunk(chunk_b)
    cot_own = to_chips(cotangent)
    got_c = gather_chunk(chunk_c)
    got_d = gather_chunk(chunk_d)
    gain_f = got_a[0][:, 3 * heads_cols : 3 * heads_cols + 3].astype(f32).T
    hc = heads_cols
    w_qkv = [g[:, : 3 * hc] for g in got_a]
    w_ot = [g[:, :hc] for g in got_b]
    w_cq = [g[:, hc : 2 * hc] for g in got_b]
    w_ckv = [g[:, 2 * hc : 4 * hc] for g in got_b]
    w_cot = [g[:, 4 * hc :] for g in got_b]
    w_gu = got_c
    w_dt = got_d
    halves = lambda v: (v[:own_rows], v[own_rows:])
    x_rows = tok_own.astype(f32)
    norm_one = both_cores(rms_norm(x_rows, gain_f[0]).astype(bf16))
    qkv = [nn(norm_one, w).astype(bf16) for w in w_qkv]
    qkv = [(t[:, :hc], t[:, hc : 2 * hc], t[:, 2 * hc :]) for t in qkv]
    self_out = [attend(q, k, v, allowed) for q, k, v in qkv]
    head_top = jnp.stack(
        [
            jnp.max(jnp.where(valid_all[None, :, None], o[2], neg_large), axis=(1, 2))
            for o in self_out
        ]
    )
    branch = nt(self_out[0][0], w_ot[0]) + nt(self_out[1][0], w_ot[1])
    hidden_one = x_rows + sum_cores(halves(branch))
    norm_two = both_cores(rms_norm(hidden_one, gain_f[1]).astype(bf16))
    enc_all = both_cores(enc_own)
    cross_q = [nn(norm_two, w).astype(bf16) for w in w_cq]
    cross_kv = [nn(enc_all, w).astype(bf16) for w in w_ckv]
    cross_kv = [(t[:, :hc], t[:, hc:]) for t in cross_kv]
    cross_out = [attend(q, k, v, True) for q, (k, v) in zip(cross_q, cross_kv)]
    branch = nt(cross_out[0][0], w_cot[0]) + nt(cross_out[1][0], w_cot[1])
    hidden_two = hidden_one + sum_cores(halves(branch))
    norm_three = both_cores(rms_norm(hidden_two, gain_f[2]).astype(bf16))
    gate_up = [nn(norm_three, w) for w in w_gu]
    gate_up = [(t[:, :hidden], t[:, hidden:]) for t in gate_up]
    inner = [gelu_product(g, u).astype(bf16) for g, u in gate_up]
    branch = nt(inner[0], w_dt[0]) + nt(inner[1], w_dt[1])
    out_rows = (hidden_two + sum_cores(halves(branch))) * valid_own
    block_output = from_chips(out_rows.astype(bf16))
    grad_out = cot_own.astype(f32) * valid_own
    grad_out_all = both_cores(grad_out.astype(bf16))
    g_dt = [tn(grad_out_all, f) for f in inner]
    red_d = reduce_chunk(*g_dt)
    grad_gu = []
    for (g, u), w in zip(gate_up, w_dt):
        _, back = jax.vjp(gelu_product, g, u)
        dg, du = back(nn(grad_out_all, w))
        grad_gu.append(jnp.concatenate([dg.astype(bf16), du.astype(bf16)], axis=1))
    g_gu = [tn(norm_three, t) for t in grad_gu]
    red_c = reduce_chunk(*g_gu)
    grad_norm = sum_cores(halves(nt(grad_gu[0], w_gu[0]) + nt(grad_gu[1], w_gu[1])))
    grad_h, gain_three = norm_back(hidden_two, gain_f[2], grad_norm)
    grad_hidden_two = grad_out + grad_h
    grad_co = both_cores(grad_hidden_two.astype(bf16))
    g_cot = [tn(grad_co, o[0]) for o in cross_out]
    grad_ca = [nn(grad_co, w).astype(bf16) for w in w_cot]
    cross_back = [
        attend_back(q, k, v, True, o[1], d)
        for q, (k, v), o, d in zip(cross_q, cross_kv, cross_out, grad_ca)
    ]
    g_cq = [tn(norm_two, b[0]) for b in cross_back]
    d_ckv = [jnp.concatenate([b[1], b[2]], axis=1) for b in cross_back]
    g_ckv = [tn(enc_all, t) for t in d_ckv]
    red_b = reduce_chunk(*[jnp.concatenate(t, axis=1) for t in zip(g_cq, g_ckv, g_cot)])
    grad_norm = sum_cores(halves(nt(cross_back[0][0], w_cq[0]) + nt(cross_back[1][0], w_cq[1])))
    grad_enc = sum_cores(halves(nt(d_ckv[0], w_ckv[0]) + nt(d_ckv[1], w_ckv[1])))
    grad_encoder = from_chips(grad_enc.astype(bf16))
    grad_h, gain_two = norm_back(hidden_one, gain_f[1], grad_norm)
    grad_hidden_one = grad_hidden_two + grad_h
    grad_o = both_cores(grad_hidden_one.astype(bf16))
    g_ot = [tn(grad_o, o[0]) for o in self_out]
    grad_a = [nn(grad_o, w).astype(bf16) for w in w_ot]
    self_back = [
        jnp.concatenate(attend_back(q, k, v, allowed, o[1], d), axis=1)
        for (q, k, v), o, d in zip(qkv, self_out, grad_a)
    ]
    g_qkv = [tn(norm_one, t) for t in self_back]
    red_a = reduce_chunk(*[jnp.concatenate(t, axis=1) for t in zip(g_qkv, g_ot)])
    grad_norm = sum_cores(halves(nt(self_back[0], w_qkv[0]) + nt(self_back[1], w_qkv[1])))
    grad_h, gain_one = norm_back(x_rows, gain_f[0], grad_norm)
    grad_tokens = from_chips((grad_hidden_one + grad_h).astype(bf16))
    gain_total = lax.psum(jnp.stack([gain_one, gain_two, gain_three]), ("mx", "mc"))
    red_gain = lax.psum_scatter(gain_total, "dp", scatter_dimension=1, tiled=True)
    mx = lax.axis_index("mx")
    local_heads = hc // DK
    head_rows = jnp.where(mx == 0, head_top, head_top[::-1])
    head_peak = lax.dynamic_index_in_dim(lax.pmax(head_rows, chips), mx, 0, keepdims=False)
    unflat = lambda t, n: jnp.swapaxes(t.reshape(model_rows, n, -1), 0, 1)
    red_in = jnp.concatenate([unflat(red_a[:, : 3 * hc], 3), unflat(red_b[:, : 3 * hc], 3)])
    red_out = jnp.stack([red_a[:, 3 * hc :].T, red_b[:, 3 * hc :].T])
    clip_factors = clip_limit / jnp.maximum(head_peak, clip_limit)
    column = jnp.repeat(jnp.sqrt(clip_factors), DK)
    factor = jnp.where((jnp.arange(6) < 2)[:, None, None], column[None, None, :], 1.0)
    grad_scale = float(seq_count * slot_len) ** (-0.5)
    up_a = apply_update(attn_in, red_in, mom_attn_in, avg_attn_in, factor, grad_scale)
    up_b = apply_update(attn_out, red_out, mom_attn_out, avg_attn_out, 1.0, grad_scale)
    up_c = apply_update(ff_in, unflat(red_c, 2), mom_ff_in, avg_ff_in, 1.0, grad_scale)
    up_d = apply_update(ff_out, red_d.T, mom_ff_out, avg_ff_out, 1.0, grad_scale)
    up_e = apply_update(gains, red_gain, mom_gains, avg_gains, 1.0, grad_scale)
    return (
        block_output,
        grad_tokens,
        grad_encoder,
        *up_a,
        *up_b,
        *up_c,
        *up_d,
        *up_e,
        head_peak,
        clip_factors,
    )


def solution(mesh):
    dp, mp = (mesh.shape["dp"], mesh.shape["mp"])
    fine = Mesh(mesh.devices.reshape(dp, mp // 2, 2), ("dp", "mx", "mc"))
    mp_axes = ("mx", "mc")
    rows = P(None, ("dp", "mx", "mc"), None)
    wide = P(None, "dp", mp_axes)
    tall = P(None, mp_axes, "dp")
    down = P(mp_axes, "dp")
    gain = P(None, "dp")
    state = (wide, tall, wide, down, gain)
    in_specs = (rows, rows, rows, P(), P(), *state, *state, *state)
    out_specs = (
        rows,
        rows,
        rows,
        *[wide] * 4,
        *[tall] * 4,
        *[wide] * 4,
        *[down] * 4,
        *[gain] * 4,
        P(mp_axes),
        P(mp_axes),
    )
    return jax.shard_map(
        on_device, mesh=fine, in_specs=in_specs, out_specs=out_specs, check_vma=False
    )
```

profile of v0, /device:TPU:0, one launch (start us, length us, event | category | flops | bytes accessed | tf_op | source)
XLA Modules:
  0.0 978.8 jit_solution(4755610367959535407)
XLA Ops:
  10.4 8.3 all-to-all-start
  19.6 30.9 %all-to-all-done = bf16[16,32,1024]{2,1,0:T(8,128)(2,1)S(1)} async-done(((bf16[16,32,1024]{2,1,0:T(8,128)(2,1)}), bf16[16,32,1024]{2,1,0:T(8,128)(2,1)S(1)}, u32[]{:S(2)}, u32[]{:S(2)}) %all-to-all-start) | async-done | bytes 1048608 | tf_op jit(solution)/shard_map/all_to_all | solution.py:147
  50.9 20.9 %all-gather.5.cloned.1.call-done = bf16[1024,896]{0,1:T(8,128)(2,1)} async-done(((bf16[128,896]{0,1:T(8,128)(2,1)}), bf16[1024,896]{0,1:T(8,128)(2,1)}) %all-gather.5.cloned.1.call-update) | async-done | bytes 1835024 | tf_op jit(solution)/shard_map/all_gather | solution.py:105
  81.4 8.2 fusion.153
  89.6 39.9 %all-gather.7.cloned.1.call-done = bf16[1024,1280]{0,1:T(8,128)(2,1)} async-done(((bf16[128,1280]{0,1:T(8,128)(2,1)}), bf16[1024,1280]{0,1:T(8,128)(2,1)}) %all-gather.7.cloned.1.call-update) | async-done | bytes 2621456 | tf_op jit(solution)/shard_map/all_gather | solution.py:105
  138.4 9.9 %select_reduce_fusion = (f32[4,1024]{1,0:T(4,128)}, f32[4,1024]{1,0:T(4,128)}, f32[4,1024,1024]{1,2,0:T(8,128)}) fusion(pred[1024,1024]{0,1:T(8,128)(4,1)S(1)} %broadcast_compare_fusion, f32[4,1024,1024]{1,2,0:T(8,128)S(1)} %copy-done, bf16[1024,4,64]{0,2,1:T(8,128)(2,1)} %bitcast.269, bf16[1024,4,64]{0,2,1:T(8,128)(2,1)} %bitcast.267), kind=kOutput, calls=%fused_computation.24 | convolution fusion | flops 553639936 | bytes 35684352 | tf_op jit(solution)/shard_map/qhe,khe->hqk/dot_general | solution.py:56
  148.3 9.1 fusion.1
  164.0 8.2 fusion.78
  172.2 15.8 %collective-permute-done.2 = bf16[1024,1280]{0,1:T(8,128)(2,1)} collective-permute-done((bf16[1024,1280]{0,1:T(8,128)(2,1)}, bf16[1024,1280]{0,1:T(8,128)(2,1)}, u32[]{:S(2)}, u32[]{:S(2)}) %collective-permute-start.2) | collective-permute-done | bytes 2621472 | tf_op jit(solution)/shard_map/ppermute | solution.py:106
  191.9 30.0 %all_to_all.24 = bf16[16,32,1024]{2,1,0:T(8,128)(2,1)} all-to-all(bf16[16,32,1024]{2,1,0:T(8,128)(2,1)S(1)} %copy-done.58), channel_id=1, replica_groups=mesh['dp'=8,'mx'=2,'mc'=2] {'dp','mx'}, dimensions={0} | all-to-all | bytes 2097152 | tf_op jit(solution)/shard_map/all_to_all | solution.py:147
  235.7 8.2 fusion.151
  243.9 8.0 fusion.2
  262.1 8.2 fusion.152
  312.1 19.2 %all-to-all-done.3 = bf16[16,32,1024]{2,1,0:T(8,128)(2,1)} async-done(((bf16[16,32,1024]{2,1,0:T(8,128)(2,1)}), bf16[16,32,1024]{2,1,0:T(8,128)(2,1)}, u32[]{:S(2)}, u32[]{:S(2)}) %all-to-all-start.3) | async-done | bytes 1048608 | tf_op jit(solution)/shard_map/all_to_all | solution.py:147
  333.8 15.6 %all-gather.11.cloned.1.call-done = bf16[1024,704]{0,1:T(8,128)(2,1)} async-done(((bf16[128,704]{0,1:T(8,128)(2,1)}), bf16[1024,704]{0,1:T(8,128)(2,1)}) %all-gather.11.cloned.1.call-update) | async-done | bytes 1441808 | tf_op jit(solution)/shard_map/all_gather | solution.py:105
  356.8 20.6 %collective-permute-done.8 = bf16[1024,1408]{0,1:T(8,128)(2,1)} collective-permute-done((bf16[1024,1408]{0,1:T(8,128)(2,1)}, bf16[1024,1408]{0,1:T(8,128)(2,1)}, u32[]{:S(2)}, u32[]{:S(2)}) %collective-permute-start.8) | collective-permute-done | bytes 2883616 | tf_op jit(solution)/shard_map/ppermute | solution.py:106
  388.7 18.6 %collective-permute-done.9 = bf16[1024,704]{0,1:T(8,128)(2,1)S(1)} collective-permute-done((bf16[1024,704]{0,1:T(8,128)(2,1)}, bf16[1024,704]{0,1:T(8,128)(2,1)S(1)}, u32[]{:S(2)}, u32[]{:S(2)}) %collective-permute-start.9) | collective-permute-done | bytes 1441824 | tf_op jit(solution)/shard_map/ppermute | solution.py:106
  440.0 11.2 %multiply_reduce_fusion.3 = (f32[4,1024]{1,0:T(4,128)}, f32[4,1024,1024]{1,2,0:T(8,128)}) fusion(f32[4,1024,1024]{1,2,0:T(8,128)S(1)} %bitcast.246, f32[4,1024]{1,0:T(4,128)S(1)} %log_add_fusion.3, bf16[1024,4,64]{0,2,1:T(8,128)(2,1)} %bitcast.282, bf16[1024,4,64]{0,2,1:T(8,128)(2,1)} %bitcast.291), kind=kOutput, calls=%fused_computation.10 | convolution fusion | flops 549449728 | bytes 34635776 | tf_op jit(solution)/shard_map/qhe,khe->hqk/dot_general | solution.py:71
  465.6 16.2 %multiply_reduce_fusion.2 = (f32[4,1024]{1,0:T(4,128)}, f32[4,1024,1024]{1,2,0:T(8,128)}) fusion(f32[4,1024,1024]{1,2,0:T(8,128)} %get-tuple-element.99, f32[4,1024]{1,0:T(4,128)S(1)} %copy-done.85, bf16[1024,4,64]{0,2,1:T(8,128)(2,1)} %bitcast.284, bf16[1024,4,64]{0,2,1:T(8,128)(2,1)} %bitcast.289), kind=kOutput, calls=%fused_computation.7 | convolution fusion | flops 549449728 | bytes 34635776 | tf_op jit(solution)/shard_map/qhe,khe->hqk/dot_general | solution.py:71
  481.7 8.1 multiply_convert_fusion.2
  514.9 21.3 %collective-permute-done.21 = bf16[1024,704]{0,1:T(8,128)(2,1)S(1)} collective-permute-done((bf16[1024,704]{0,1:T(8,128)(2,1)S(1)}, bf16[1024,704]{0,1:T(8,128)(2,1)S(1)}, u32[]{:S(2)}, u32[]{:S(2)}) %collective-permute-start.21) | collective-permute-done | bytes 1441824 | tf_op jit(solution)/shard_map/ppermute | solution.py:110
  543.9 8.3 fusion.155
  570.9 24.6 %multiply_reduce_fusion = (f32[4,1024]{1,0:T(4,128)S(1)}, f32[4,1024]{1,0:T(4,128)S(1)}, f32[4,1024,1024]{1,2,0:T(8,128)}) fusion(f32[4,1024,1024]{1,2,0:T(8,128)} %get-tuple-element.95, f32[4,1024]{1,0:T(4,128)S(1)} %log_add_fusion, pred[1024,1024]{0,1:T(8,128)(4,1)S(1)} %copy-done.4, f32[4,1024,1024]{1,2,0:T(8,128)} %fusion.155, ...), kind=kOutput, calls=%fused_computation.1 | convolution fusion | flops 570417152 | bytes 69271552 | tf_op jit(solution)/shard_map/qhe,khe->hqk/dot_general | solution.py:71
  595.6 29.9 %multiply_convert_fusion = (bf16[4,1024,1024]{1,2,0:T(8,128)(2,1)}, bf16[4,1024,1024]{1,2,0:T(8,128)(2,1)}) fusion(f32[4,1024,1024]{1,2,0:T(8,128)} %get-tuple-element.104, f32[4,1024,1024]{1,2,0:T(8,128)} %get-tuple-element.95, f32[4,1024]{1,0:T(4,128)S(1)} %get-tuple-element.31, f32[4,1024]{1,0:T(4,128)S(1)} %log_add_fusion, ...), kind=kLoop, calls=%fused_computation | loop fusion | flops 41943040 | bytes 85000192 | tf_op jit(solution)/shard_map/convert_element_type | solution.py:76
  653.9 8.1 add_convert_fusion
  669.1 8.8 fusion.75
  700.7 32.4 %collective-permute-done.19 = bf16[1024,1024]{0,1:T(8,128)(2,1)} collective-permute-done((bf16[1024,1024]{0,1:T(8,128)(2,1)}, bf16[1024,1024]{0,1:T(8,128)(2,1)}, u32[]{:S(2)}, u32[]{:S(2)}) %collective-permute-start.19) | collective-permute-done | bytes 2097184 | tf_op jit(solution)/shard_map/ppermute | solution.py:110
  779.7 22.5 %collective-permute-done.18 = bf16[1024,1024]{0,1:T(8,128)(2,1)} collective-permute-done((bf16[1024,1024]{0,1:T(8,128)(2,1)}, bf16[1024,1024]{0,1:T(8,128)(2,1)}, u32[]{:S(2)}, u32[]{:S(2)}) %collective-permute-start.18) | collective-permute-done | bytes 2097184 | tf_op jit(solution)/shard_map/ppermute | solution.py:110
  812.8 9.2 reduce.6
  843.0 15.5 %all-to-all-done.5 = bf16[16,2,16384]{2,1,0:T(2,128)(2,1)} async-done(((bf16[16,2,16384]{2,1,0:T(2,128)(2,1)}), bf16[16,2,16384]{2,1,0:T(2,128)(2,1)}, u32[]{:S(2)}, u32[]{:S(2)}) %all-to-all-start.5) | async-done | bytes 1048608 | tf_op jit(solution)/shard_map/all_to_all | solution.py:151
  865.4 57.6 %pmax.7 = f32[2,4]{1,0:T(2,128)S(1)} all-reduce(f32[2,4]{1,0:T(2,128)S(1)} %broadcast_select_fusion.1), channel_id=1, replica_groups=mesh['dp'=8,'mx'=2,'mc'=2] {'dp','mx'}, use_global_device_ids=true, to_apply=%region_22.23 | all-reduce | flops 8 | bytes 64 | tf_op jit(solution)/shard_map/pmax | solution.py:264
  956.5 8.9 reduce-scatter.16.cloned.1.call-done
  (569 shorter events, 397.9 us)
Async XLA Ops:
  7.2 64.6 %all-gather.5.cloned.1.call-start = ((), (), s32[]{:S(2)}) async-start(), calls=%async_computation.11 | async-start | bytes 2064384 | tf_op jit(solution)/shard_map/all_gather | solution.py:105
  10.4 40.1 %all-to-all-start = ((bf16[16,32,1024]{2,1,0:T(8,128)(2,1)}), bf16[16,32,1024]{2,1,0:T(8,128)(2,1)S(1)}, u32[]{:S(2)}, u32[]{:S(2)}) async-start(bf16[16,32,1024]{2,1,0:T(8,128)(2,1)} %param.20), calls=%async_computation | async-start | bytes 2097152 | tf_op jit(solution)/shard_map/all_to_all | solution.py:147
  18.7 110.8 %all-gather.7.cloned.1.call-start = ((), (), s32[]{:S(2)}) async-start(), calls=%async_computation.12 | async-start | bytes 2949120 | tf_op jit(solution)/shard_map/all_gather | solution.py:105
  19.6 281.5 %all-gather.9.cloned.1.call-start = ((), (), s32[]{:S(2)}) async-start(), calls=%async_computation.13 | async-start | bytes 3244032 | tf_op jit(solution)/shard_map/all_gather | solution.py:105
  74.1 56.9 %collective-permute-start.1 = (bf16[1024,896]{0,1:T(8,128)(2,1)}, bf16[1024,896]{0,1:T(8,128)(2,1)}, u32[]{:S(2)}, u32[]{:S(2)}) collective-permute-start(bf16[1024,896]{0,1:T(8,128)(2,1)} %all-gather.5.cloned.1.call-done), channel_id=1, source_target_pairs={{0,2},{2,0},{1,3},{3,1},{4,6},{6,4},{5,7},{7,5},{8,10},{10,8},{9,1... | collective-permute-start | bytes 5505032 | tf_op jit(solution)/shard_map/ppermute | solution.py:106
  129.5 58.5 %collective-permute-start.2 = (bf16[1024,1280]{0,1:T(8,128)(2,1)}, bf16[1024,1280]{0,1:T(8,128)(2,1)}, u32[]{:S(2)}, u32[]{:S(2)}) collective-permute-start(bf16[1024,1280]{0,1:T(8,128)(2,1)} %all-gather.7.cloned.1.call-done), channel_id=1, source_target_pairs={{0,2},{2,0},{1,3},{3,1},{4,6},{6,4},{5,7},{7,5},{8,10},{10,8},{9,1... | collective-permute-start | bytes 7864328 | tf_op jit(solution)/shard_map/ppermute | solution.py:106
  190.0 32.9 %collective-permute-start.3 = (f32[512,1024]{1,0:T(8,128)S(1)}, f32[512,1024]{1,0:T(8,128)}, u32[]{:S(2)}, u32[]{:S(2)}) collective-permute-start(f32[512,1024]{1,0:T(8,128)S(1)} %slice.222), channel_id=1, source_target_pairs={{0,1},{1,0},{2,3},{3,2},{4,5},{5,4},{6,7},{7,6},{8,9},{9,8},{10,11... | collective-permute-start | bytes 6291464 | tf_op jit(solution)/shard_map/ppermute | solution.py:47
  221.9 4.9 collective-permute-start.4
  222.7 126.7 %all-gather.11.cloned.1.call-start = ((), (), s32[]{:S(2)}) async-start(), calls=%async_computation.14 | async-start | bytes 1622016 | tf_op jit(solution)/shard_map/all_gather | solution.py:105
  226.2 8.5 collective-permute-start.5
  295.3 7.6 collective-permute-start.6
  296.5 34.8 %all-to-all-start.3 = ((bf16[16,32,1024]{2,1,0:T(8,128)(2,1)}), bf16[16,32,1024]{2,1,0:T(8,128)(2,1)}, u32[]{:S(2)}, u32[]{:S(2)}) async-start(bf16[16,32,1024]{2,1,0:T(8,128)(2,1)} %param.22), calls=%async_computation.3 | async-start | bytes 2097152 | tf_op jit(solution)/shard_map/all_to_all | solution.py:147
  300.8 629.1 %reduce-scatter.20.cloned.1.call-start = ((), (), s32[]{:S(2)}) async-start(), calls=%async_computation.18 | async-start | bytes 1769472
  301.1 76.3 %collective-permute-start.8 = (bf16[1024,1408]{0,1:T(8,128)(2,1)}, bf16[1024,1408]{0,1:T(8,128)(2,1)}, u32[]{:S(2)}, u32[]{:S(2)}) collective-permute-start(bf16[1024,1408]{0,1:T(8,128)(2,1)} %all-gather.9.cloned.1.call-done), channel_id=1, source_target_pairs={{0,2},{2,0},{1,3},{3,1},{4,6},{6,4},{5,7},{7,5},{8,10},{10,8},{9,1... | collective-permute-start | bytes 8650760 | tf_op jit(solution)/shard_map/ppermute | solution.py:106
  308.3 42.6 %collective-permute-start.7 = (bf16[512,1024]{1,0:T(8,128)(2,1)}, bf16[512,1024]{1,0:T(8,128)(2,1)}, u32[]{:S(2)}, u32[]{:S(2)}) collective-permute-start(bf16[512,1024]{1,0:T(8,128)(2,1)} %multiply_convert_fusion.8), channel_id=1, source_target_pairs={{0,1},{1,0},{2,3},{3,2},{4,5},{5,4},{6,7},{7,6},{8,9},{9,8},{10,11... | collective-permute-start | bytes 3145736 | tf_op jit(solution)/shard_map/ppermute | solution.py:42
  333.8 49.6 %collective-permute-start.11 = (bf16[512,1024]{1,0:T(8,128)(2,1)}, bf16[512,1024]{1,0:T(8,128)(2,1)}, u32[]{:S(2)}, u32[]{:S(2)}) collective-permute-start(bf16[512,1024]{1,0:T(8,128)(2,1)} %fusion.47), channel_id=1, source_target_pairs={{0,1},{1,0},{2,3},{3,2},{4,5},{5,4},{6,7},{7,6},{8,9},{9,8},{10,11... | collective-permute-start | bytes 3145736 | tf_op jit(solution)/shard_map/ppermute | solution.py:42
  349.4 57.9 %collective-permute-start.9 = (bf16[1024,704]{0,1:T(8,128)(2,1)}, bf16[1024,704]{0,1:T(8,128)(2,1)S(1)}, u32[]{:S(2)}, u32[]{:S(2)}) collective-permute-start(bf16[1024,704]{0,1:T(8,128)(2,1)} %all-gather.11.cloned.1.call-done), channel_id=1, source_target_pairs={{0,2},{2,0},{1,3},{3,1},{4,6},{6,4},{5,7},{7,5},{8,10},{10,8},{9,1... | collective-permute-start | bytes 4325384 | tf_op jit(solution)/shard_map/ppermute | solution.py:106
  421.9 4.6 collective-permute-start.12
  497.3 5.0 collective-permute-start.14
  501.7 34.5 %collective-permute-start.21 = (bf16[1024,704]{0,1:T(8,128)(2,1)S(1)}, bf16[1024,704]{0,1:T(8,128)(2,1)S(1)}, u32[]{:S(2)}, u32[]{:S(2)}) collective-permute-start(bf16[1024,704]{0,1:T(8,128)(2,1)S(1)} %convolution_convert_fusion.4), channel_id=1, source_target_pairs={{0,2},{2,0},{1,3},{3,1},{4,6},{6,4},{5,7},{7,5},{8,10},{10,8},{9,1... | collective-permute-start | bytes 4325384 | tf_op jit(solution)/shard_map/ppermute | solution.py:110
  505.6 35.8 %collective-permute-start.15 = (bf16[512,1024]{1,0:T(8,128)(2,1)}, bf16[512,1024]{1,0:T(8,128)(2,1)S(1)}, u32[]{:S(2)}, u32[]{:S(2)}) collective-permute-start(bf16[512,1024]{1,0:T(8,128)(2,1)} %get-tuple-element.61), channel_id=1, source_target_pairs={{0,1},{1,0},{2,3},{3,2},{4,5},{5,4},{6,7},{7,6},{8,9},{9,8},{10,11... | collective-permute-start | bytes 3145736 | tf_op jit(solution)/shard_map/ppermute | solution.py:42
  513.7 140.2 %collective-permute-start.20 = (bf16[1024,1408]{1,0:T(8,128)(2,1)}, bf16[1024,1408]{1,0:T(8,128)(2,1)}, u32[]{:S(2)}, u32[]{:S(2)}) collective-permute-start(bf16[1024,1408]{1,0:T(8,128)(2,1)} %convolution_convert_fusion), channel_id=1, source_target_pairs={{0,2},{2,0},{1,3},{3,1},{4,6},{6,4},{5,7},{7,5},{8,10},{10,8},{9,1... | collective-permute-start | bytes 8650760 | tf_op jit(solution)/shard_map/ppermute | solution.py:110
  541.1 398.4 %reduce-scatter.22.cloned.1.call-start = ((), (), s32[]{:S(2)}) async-start(), calls=%async_computation.19 | async-start | bytes 589824
  653.6 293.3 %reduce-scatter.14.cloned.1.call-start = ((), (), s32[]{:S(2)}) async-start(), calls=%async_computation.15 | async-start | bytes 3244032 | tf_op jit(solution)/shard_map/reduce_scatter | solution.py:112
  662.0 289.6 %reduce-scatter.18.cloned.1.call-start = ((), (), s32[]{:S(2)}) async-start(), calls=%async_computation.17 | async-start | bytes 2359296
  685.2 48.0 %collective-permute-start.19 = (bf16[1024,1024]{0,1:T(8,128)(2,1)}, bf16[1024,1024]{0,1:T(8,128)(2,1)}, u32[]{:S(2)}, u32[]{:S(2)}) collective-permute-start(bf16[1024,1024]{0,1:T(8,128)(2,1)} %pad_maximum_fusion.10), channel_id=1, source_target_pairs={{0,2},{2,0},{1,3},{3,1},{4,6},{6,4},{5,7},{7,5},{8,10},{10,8},{9,1... | collective-permute-start | bytes 6291464 | tf_op jit(solution)/shard_map/ppermute | solution.py:110
  748.0 54.2 %collective-permute-start.18 = (bf16[1024,1024]{0,1:T(8,128)(2,1)}, bf16[1024,1024]{0,1:T(8,128)(2,1)}, u32[]{:S(2)}, u32[]{:S(2)}) collective-permute-start(bf16[1024,1024]{0,1:T(8,128)(2,1)} %pad_maximum_fusion.9), channel_id=1, source_target_pairs={{0,2},{2,0},{1,3},{3,1},{4,6},{6,4},{5,7},{7,5},{8,10},{10,8},{9,1... | collective-permute-start | bytes 6291464 | tf_op jit(solution)/shard_map/ppermute | solution.py:110
  754.7 52.6 %collective-permute-start.17 = (f32[512,1024]{1,0:T(8,128)}, f32[512,1024]{1,0:T(8,128)}, u32[]{:S(2)}, u32[]{:S(2)}) collective-permute-start(f32[512,1024]{1,0:T(8,128)} %slice.250), channel_id=1, source_target_pairs={{0,1},{1,0},{2,3},{3,2},{4,5},{5,4},{6,7},{7,6},{8,9},{9,8},{10,11... | collective-permute-start | bytes 6291464 | tf_op jit(solution)/shard_map/ppermute | solution.py:47
  767.6 56.9 %all-to-all-start.2 = ((bf16[16,2,16384]{2,1,0:T(2,128)(2,1)}), bf16[16,2,16384]{2,1,0:T(2,128)(2,1)}, u32[]{:S(2)}, u32[]{:S(2)}) async-start(bf16[16,2,16384]{2,1,0:T(2,128)(2,1)} %reshape.470), calls=%async_computation.2 | async-start | bytes 2097152 | tf_op jit(solution)/shard_map/all_to_all | solution.py:151
  774.2 191.2 %reduce-scatter.16.cloned.1.call-start = ((), (), s32[]{:S(2)}) async-start(), calls=%async_computation.16 | async-start | bytes 2359296
  824.6 33.9 %all-to-all-start.5 = ((bf16[16,2,16384]{2,1,0:T(2,128)(2,1)}), bf16[16,2,16384]{2,1,0:T(2,128)(2,1)}, u32[]{:S(2)}, u32[]{:S(2)}) async-start(bf16[16,2,16384]{2,1,0:T(2,128)(2,1)} %reshape.474), calls=%async_computation.5 | async-start | bytes 2097152 | tf_op jit(solution)/shard_map/all_to_all | solution.py:151
  858.5 95.2 %all-to-all-start.4 = ((bf16[16,2,16384]{2,1,0:T(2,128)(2,1)}), bf16[16,2,16384]{2,1,0:T(2,128)(2,1)S(1)}, u32[]{:S(2)}, u32[]{:S(2)}) async-start(bf16[16,2,16384]{2,1,0:T(2,128)(2,1)} %reshape.472), calls=%async_computation.4 | async-start | bytes 2097152 | tf_op jit(solution)/shard_map/all_to_all | solution.py:151
  (170 other events, 1768.2 us)
Sparse Core Ops, SparseCore 0:
  10.7 61.0 all-gather.4
  74.4 55.0 all-gather.6
  222.8 58.4 all-gather.8
  296.6 52.7 all-gather.10
  541.3 64.9 reduce-scatter.19
  653.7 62.0 reduce-scatter.21
  719.3 86.9 reduce-scatter.13
  809.8 84.6 reduce-scatter.17
  898.1 67.2 reduce-scatter.15
where the time goes:
time: 987 us; the launch traced here: 979 us
  matrix products  311 us (32%)
  waiting for transfers between devices  290 us (29%)
  other arithmetic  148 us (15%)
  blocking collectives  93.6 us (9%)
  local copies, waits for them, and re-layouts  72.8 us (7%)
  starting transfers between devices  44.2 us (4%)
  between operations  18.7 us (2%)
    all_gather x4, waiting for transfers between devices, gather_chunk(): own = lax.all_gather(local, 'dp', axis=0, tiled=True)  76.4 us
    ppermute x4, waiting for transfers between devices, reduce_chunk(): arrived = lax.ppermute(other.astype(bf16), 'mx', swap)  76.2 us
    dot_general x4, matrix products, attend_back(): jnp.einsum('qhe,khe->hqk', grad_h, values_h, preferred_element_type=f32)  60.3 us
    pmax x1, blocking collectives, on_device(): lax.pmax(head_rows, chips)  57.6 us
    unnamed x351, local copies, waits for them, and re-layouts  57 us
    ppermute x4, waiting for transfers between devices, gather_chunk(): return (own, lax.ppermute(own, 'mx', swap))  55.1 us
    dot_general x14, matrix products, nn(): lax.dot_general(left, right, (((1,), (0,)), ((), ())), preferred_element_...  50.1 us
    all_to_all x2, waiting for transfers between devices, to_chips(): lax.all_to_all(values, chips, split_axis=0, concat_axis=1, tiled=True)  50.1 us
  transfers between devices with their start and end apart: 36, of which 17 were waited for; matrix products, arithmetic and copies ran while one was open for 43% of the time, Pallas kernels for 0%

commit v1 on v0

--- a/solution.py
+++ b/solution.py
@@ -17,6 +17,28 @@
 chips = ("dp", "mx")
 
 
+def laid_out(blocks, dim):
+    shape = list(blocks.shape[1:])
+    shape[dim] *= blocks.shape[0]
+    return jnp.moveaxis(blocks, 0, dim).reshape(shape)
+
+
+def ring_gather(shard, axis, dim):
+    count = lax.axis_size(axis)
+    pairs = [(i, (i + 1) % count) for i in range(count)]
+    back = [(b, a) for a, b in pairs]
+    lower, upper = ([], [])
+    for turn in range(count - 1):
+        if turn % 2 == 0:
+            lower.append(lax.ppermute(lower[-1] if lower else shard, axis, pairs))
+        else:
+            upper.append(lax.ppermute(upper[-1] if upper else shard, axis, back))
+    pieces = jnp.stack([*lower[::-1], shard, *upper])
+    shift = lax.axis_index(axis) - len(lower)
+    pieces = pieces[(jnp.arange(count) - shift) % count]
+    return laid_out(pieces, dim)
+
+
 def rms_norm(hidden, gain_vec):
     row_scale = lax.rsqrt(jnp.mean(hidden * hidden, axis=-1, keepdims=True) + epsilon)
     return hidden * row_scale * gain_vec
@@ -102,7 +124,7 @@
 
 
 def gather_chunk(local):
-    own = lax.all_gather(local, "dp", axis=0, tiled=True)
+    own = ring_gather(local, "dp", 0)
     return (own, lax.ppermute(own, "mx", swap))
 
 

time: 987 us -> 1070 us (1.084)
  local copies, waits for them, and re-layouts: 72.8 us -> 138 us
  starting transfers between devices: 44.2 us -> 99.7 us
  blocking collectives: 93.6 us -> 61.8 us
    ppermute x0 -> x28, waiting for transfers between devices: none -> 104 us  [the longest x16 66.8 us: ring_gather(): lower.append(lax.ppermute(lower[-1] if lower else shard, axis, pairs))]
    all_gather x4 -> x0, waiting for transfers between devices: 76.4 us -> none  [gather_chunk(): own = lax.all_gather(local, 'dp', axis=0, tiled=True)]
    ppermute x0 -> x28, starting transfers between devices: none -> 52.1 us  [the longest x12 33.5 us: ring_gather(): upper.append(lax.ppermute(upper[-1] if upper else shard, axis, back))]
    all_to_all x2 -> x3, waiting for transfers between devices: 50.1 us -> 0.01 us  [to_chips(): lax.all_to_all(values, chips, split_axis=0, concat_axis=1, tiled=True)]
    unnamed x351 -> x412, local copies, waits for them, and re-layouts: 57 us -> 87 us
    all_to_all x1 -> x0, blocking collectives: 30 us -> none  [to_chips(): lax.all_to_all(values, chips, split_axis=0, concat_axis=1, tiled=True)]
    gather x0 -> x6, local copies, waits for them, and re-layouts: none -> 24.1 us  [ring_gather(): pieces = pieces[(jnp.arange(count) - shift) % count]]
    ppermute x4, waiting for transfers between devices: 55.1 us -> 70.4 us  [gather_chunk(): return (own, lax.ppermute(own, 'mx', swap))]
  transfers between devices with their start and end apart: 36 -> 61, of which waited for: 17 -> 22; matrix products, arithmetic and copies ran while one was open for 43% -> 46% of each run, Pallas kernels for 0% -> 0%
where the time goes in v1:
time: 1070 us; the launch traced here: 1060 us
  matrix products  307 us (29%)
  waiting for transfers between devices  283 us (26%)
  other arithmetic  152 us (14%)
  local copies, waits for them, and re-layouts  138 us (13%)
  starting transfers between devices  99.7 us (9%)
  blocking collectives  61.8 us (6%)
  between operations  18.9 us (2%)
    unnamed x412, local copies, waits for them, and re-layouts  87 us
    ppermute x4, waiting for transfers between devices, reduce_chunk(): arrived = lax.ppermute(other.astype(bf16), 'mx', swap)  73.8 us
    ppermute x4, waiting for transfers between devices, gather_chunk(): return (own, lax.ppermute(own, 'mx', swap))  70.4 us
    ppermute x16, waiting for transfers between devices, ring_gather(): lower.append(lax.ppermute(lower[-1] if lower else shard, axis, pairs))  66.8 us
    dot_general x4, matrix products, attend_back(): jnp.einsum('qhe,khe->hqk', grad_h, values_h, preferred_element_type=f32)  60.4 us
    pmax x1, blocking collectives, on_device(): lax.pmax(head_rows, chips)  55.8 us
    dot_general x14, matrix products, nn(): lax.dot_general(left, right, (((1,), (0,)), ((), ())), preferred_element_...  49.9 us
    convert_element_type x3, other arithmetic, attend_back(): grad_scores = (soft_rows * (grad_soft - row_dot)).astype(bf16)  46.1 us
  transfers between devices with their start and end apart: 61, of which 22 were waited for; matrix products, arithmetic and copies ran while one was open for 46% of the time, Pallas kernels for 0%

profile of v1, /device:TPU:0, one launch (start us, length us, event | category | flops | bytes accessed | tf_op | source)
XLA Modules:
  0.0 1059.8 jit_solution(10537528874189601579)
XLA Ops:
  36.1 28.5 %collective-permute-done.30 = bf16[128,704]{0,1:T(8,128)(2,1)} collective-permute-done((bf16[128,704]{0,1:T(8,128)(2,1)S(1)}, bf16[128,704]{0,1:T(8,128)(2,1)}, u32[]{:S(2)}, u32[]{:S(2)}) %collective-permute-start.30) | collective-permute-done | bytes 180256 | tf_op jit(solution)/shard_map/ppermute | solution.py:33
  82.0 10.1 collective-permute-done.32
  96.7 9.4 collective-permute-done.5
  122.7 14.6 %collective-permute-done.6 = bf16[128,896]{0,1:T(8,128)(2,1)S(1)} collective-permute-done((bf16[128,896]{0,1:T(8,128)(2,1)S(1)}, bf16[128,896]{0,1:T(8,128)(2,1)S(1)}, u32[]{:S(2)}, u32[]{:S(2)}) %collective-permute-start.6) | collective-permute-done | bytes 229408 | tf_op jit(solution)/shard_map/ppermute | solution.py:35
  181.1 12.8 %collective-permute-done.27 = bf16[128,1408]{1,0:T(8,128)(2,1)} collective-permute-done((bf16[128,1408]{1,0:T(8,128)(2,1)S(1)}, bf16[128,1408]{1,0:T(8,128)(2,1)}, u32[]{:S(2)}, u32[]{:S(2)}) %collective-permute-start.27) | collective-permute-done | bytes 360480 | tf_op jit(solution)/shard_map/ppermute | solution.py:35
  197.9 9.4 collective-permute-done.23
  232.6 11.2 %select_reduce_fusion = (f32[4,1024]{1,0:T(4,128)}, f32[4,1024]{1,0:T(4,128)}, f32[4,1024,1024]{1,2,0:T(8,128)}) fusion(pred[1024,1024]{0,1:T(8,128)(4,1)S(1)} %broadcast_compare_fusion, f32[4,1024,1024]{1,2,0:T(8,128)S(1)} %fusion.155, bf16[1024,4,64]{0,2,1:T(8,128)(2,1)} %bitcast.358, bf16[1024,4,64]{0,2,1:T(8,128)(2,1)} %bitcast.356), kind=kOutput, calls=%fused_computation.28 | convolution fusion | flops 553639936 | bytes 35684352 | tf_op jit(solution)/shard_map/qhe,khe->hqk/dot_general | solution.py:78
  243.8 9.1 fusion.1
  259.5 8.3 fusion.78
  267.9 10.6 collective-permute-done.16
  286.8 9.1 collective-permute-done.25
  318.4 8.2 fusion.153
  326.6 8.1 fusion.2
  347.0 8.1 fusion.154
  411.8 40.6 %collective-permute-done.36 = bf16[1024,1408]{1,0:T(8,128)(2,1)} collective-permute-done((bf16[1024,1408]{1,0:T(8,128)(2,1)}, bf16[1024,1408]{1,0:T(8,128)(2,1)}, u32[]{:S(2)}, u32[]{:S(2)}) %collective-permute-start.36) | collective-permute-done | bytes 2883616 | tf_op jit(solution)/shard_map/ppermute | solution.py:128
  463.1 19.2 %collective-permute-done.37 = bf16[1024,704]{0,1:T(8,128)(2,1)} collective-permute-done((bf16[1024,704]{0,1:T(8,128)(2,1)}, bf16[1024,704]{0,1:T(8,128)(2,1)}, u32[]{:S(2)}, u32[]{:S(2)}) %collective-permute-start.37) | collective-permute-done | bytes 1441824 | tf_op jit(solution)/shard_map/ppermute | solution.py:128
  518.9 11.2 %multiply_reduce_fusion.3 = (f32[4,1024]{1,0:T(4,128)}, f32[4,1024,1024]{1,2,0:T(8,128)}) fusion(f32[4,1024,1024]{1,2,0:T(8,128)S(1)} %bitcast.326, f32[4,1024]{1,0:T(4,128)S(1)} %log_add_fusion.3, bf16[1024,4,64]{0,2,1:T(8,128)(2,1)} %bitcast.378, bf16[1024,4,64]{0,2,1:T(8,128)(2,1)} %bitcast.386), kind=kOutput, calls=%fused_computation.14 | convolution fusion | flops 549449728 | bytes 34635776 | tf_op jit(solution)/shard_map/qhe,khe->hqk/dot_general | solution.py:93
  548.1 16.1 %multiply_reduce_fusion.2 = (f32[4,1024]{1,0:T(4,128)}, f32[4,1024,1024]{1,2,0:T(8,128)}) fusion(f32[4,1024,1024]{1,2,0:T(8,128)} %get-tuple-element.99, f32[4,1024]{1,0:T(4,128)S(1)} %copy-done.96, bf16[1024,4,64]{0,2,1:T(8,128)(2,1)} %bitcast.380, bf16[1024,4,64]{0,2,1:T(8,128)(2,1)} %bitcast.384), kind=kOutput, calls=%fused_computation.11 | convolution fusion | flops 549449728 | bytes 34635776 | tf_op jit(solution)/shard_map/qhe,khe->hqk/dot_general | solution.py:93
  564.2 8.4 multiply_convert_fusion.2
  597.2 20.8 %collective-permute-done.49 = bf16[1024,704]{0,1:T(8,128)(2,1)S(1)} collective-permute-done((bf16[1024,704]{0,1:T(8,128)(2,1)S(1)}, bf16[1024,704]{0,1:T(8,128)(2,1)S(1)}, u32[]{:S(2)}, u32[]{:S(2)}) %collective-permute-start.49) | collective-permute-done | bytes 1441824 | tf_op jit(solution)/shard_map/ppermute | solution.py:132
  624.2 8.2 fusion.156
  643.1 8.1 fusion.69
  651.2 24.8 %multiply_reduce_fusion = (f32[4,1024]{1,0:T(4,128)S(1)}, f32[4,1024]{1,0:T(4,128)S(1)}, f32[4,1024,1024]{1,2,0:T(8,128)}) fusion(f32[4,1024,1024]{1,2,0:T(8,128)} %get-tuple-element.95, f32[4,1024]{1,0:T(4,128)S(1)} %log_add_fusion, pred[1024,1024]{0,1:T(8,128)(4,1)S(1)} %copy-done.4, f32[4,1024,1024]{1,2,0:T(8,128)} %fusion.156, ...), kind=kOutput, calls=%fused_computation.5 | convolution fusion | flops 570417152 | bytes 69271552 | tf_op jit(solution)/shard_map/qhe,khe->hqk/dot_general | solution.py:93
  676.0 29.7 %multiply_convert_fusion = (bf16[4,1024,1024]{1,2,0:T(8,128)(2,1)}, bf16[4,1024,1024]{1,2,0:T(8,128)(2,1)}) fusion(f32[4,1024,1024]{1,2,0:T(8,128)} %get-tuple-element.104, f32[4,1024,1024]{1,2,0:T(8,128)} %get-tuple-element.95, f32[4,1024]{1,0:T(4,128)S(1)} %get-tuple-element.31, f32[4,1024]{1,0:T(4,128)S(1)} %log_add_fusion, ...), kind=kLoop, calls=%fused_computation.4 | loop fusion | flops 41943040 | bytes 85000192 | tf_op jit(solution)/shard_map/convert_element_type | solution.py:98
  734.1 8.1 add_convert_fusion
  749.4 8.8 fusion.75
  781.3 31.9 %collective-permute-done.47 = bf16[1024,1024]{0,1:T(8,128)(2,1)} collective-permute-done((bf16[1024,1024]{0,1:T(8,128)(2,1)}, bf16[1024,1024]{0,1:T(8,128)(2,1)}, u32[]{:S(2)}, u32[]{:S(2)}) %collective-permute-start.47) | collective-permute-done | bytes 2097184 | tf_op jit(solution)/shard_map/ppermute | solution.py:132
  838.3 8.2 reduce.10
  860.6 21.1 %collective-permute-done.46 = bf16[1024,1024]{0,1:T(8,128)(2,1)} collective-permute-done((bf16[1024,1024]{0,1:T(8,128)(2,1)}, bf16[1024,1024]{0,1:T(8,128)(2,1)}, u32[]{:S(2)}, u32[]{:S(2)}) %collective-permute-start.46) | collective-permute-done | bytes 2097184 | tf_op jit(solution)/shard_map/ppermute | solution.py:132
  921.0 18.0 %all-to-all-done.5 = bf16[16,2,16384]{2,1,0:T(2,128)(2,1)} async-done(((bf16[16,2,16384]{2,1,0:T(2,128)(2,1)}), bf16[16,2,16384]{2,1,0:T(2,128)(2,1)}, u32[]{:S(2)}, u32[]{:S(2)}) %all-to-all-start.5) | async-done | bytes 1048608 | tf_op jit(solution)/shard_map/all_to_all | solution.py:173
  945.8 55.8 %pmax.7 = f32[2,4]{1,0:T(2,128)S(1)} all-reduce(f32[2,4]{1,0:T(2,128)S(1)} %broadcast_select_fusion.1), channel_id=1, replica_groups=mesh['dp'=8,'mx'=2,'mc'=2] {'dp','mx'}, use_global_device_ids=true, to_apply=%region_22.23 | all-reduce | flops 8 | bytes 64 | tf_op jit(solution)/shard_map/pmax | solution.py:286
  1037.0 9.5 reduce-scatter.16.cloned.1.call-done
  (693 shorter events, 535.2 us)
Async XLA Ops:
  8.9 109.1 %collective-permute-start.33 = (bf16[128,704]{0,1:T(8,128)(2,1)}, bf16[128,704]{0,1:T(8,128)(2,1)}, u32[]{:S(2)}, u32[]{:S(2)}) collective-permute-start(bf16[128,704]{0,1:T(8,128)(2,1)} %convert_bitcast_fusion.2), channel_id=1, source_target_pairs={{4,0},{8,4},{12,8},{16,12},{20,16},{24,20},{28,24},{0,28},{5,1},{9... | collective-permute-start | bytes 540680 | tf_op jit(solution)/shard_map/ppermute | solution.py:35
  18.6 56.8 %collective-permute-start.4 = (bf16[128,896]{0,1:T(8,128)(2,1)}, bf16[128,896]{0,1:T(8,128)(2,1)}, u32[]{:S(2)}, u32[]{:S(2)}) collective-permute-start(bf16[128,896]{0,1:T(8,128)(2,1)} %maximum_maximum_fusion), channel_id=1, source_target_pairs={{4,0},{8,4},{12,8},{16,12},{20,16},{24,20},{28,24},{0,28},{5,1},{9... | collective-permute-start | bytes 688136 | tf_op jit(solution)/shard_map/ppermute | solution.py:35
  23.3 138.8 %all-to-all-start = ((bf16[16,32,1024]{2,1,0:T(8,128)(2,1)}), bf16[16,32,1024]{2,1,0:T(8,128)(2,1)S(1)}, u32[]{:S(2)}, u32[]{:S(2)}) async-start(bf16[16,32,1024]{2,1,0:T(8,128)(2,1)} %param.20), calls=%async_computation | async-start | bytes 2097152 | tf_op jit(solution)/shard_map/all_to_all | solution.py:169
  31.2 48.8 %collective-permute-start.8 = (bf16[128,1280]{0,1:T(8,128)(2,1)}, bf16[128,1280]{0,1:T(8,128)(2,1)}, u32[]{:S(2)}, u32[]{:S(2)}) collective-permute-start(bf16[128,1280]{0,1:T(8,128)(2,1)} %pad_maximum_fusion.27), channel_id=1, source_target_pairs={{0,4},{4,8},{8,12},{12,16},{16,20},{20,24},{24,28},{28,0},{1,5},{5... | collective-permute-start | bytes 983048 | tf_op jit(solution)/shard_map/ppermute | solution.py:33
  75.4 45.5 %collective-permute-start.12 = (bf16[128,1280]{0,1:T(8,128)(2,1)}, bf16[128,1280]{0,1:T(8,128)(2,1)}, u32[]{:S(2)}, u32[]{:S(2)}) collective-permute-start(bf16[128,1280]{0,1:T(8,128)(2,1)} %pad_maximum_fusion.27), channel_id=1, source_target_pairs={{4,0},{8,4},{12,8},{16,12},{20,16},{24,20},{28,24},{0,28},{5,1},{9... | collective-permute-start | bytes 983048 | tf_op jit(solution)/shard_map/ppermute | solution.py:35
  106.1 63.9 %collective-permute-start.26 = (bf16[128,1408]{1,0:T(8,128)(2,1)}, bf16[128,1408]{1,0:T(8,128)(2,1)S(1)}, u32[]{:S(2)}, u32[]{:S(2)}) collective-permute-start(bf16[128,1408]{1,0:T(8,128)(2,1)} %copy.162), channel_id=1, source_target_pairs={{4,0},{8,4},{12,8},{16,12},{20,16},{24,20},{28,24},{0,28},{5,1},{9... | collective-permute-start | bytes 1081352 | tf_op jit(solution)/shard_map/ppermute | solution.py:35
  106.2 39.1 %collective-permute-start.10 = (bf16[128,1280]{0,1:T(8,128)(2,1)S(1)}, bf16[128,1280]{0,1:T(8,128)(2,1)}, u32[]{:S(2)}, u32[]{:S(2)}) collective-permute-start(bf16[128,1280]{0,1:T(8,128)(2,1)S(1)} %collective-permute-done.9), channel_id=1, source_target_pairs={{0,4},{4,8},{8,12},{12,16},{16,20},{20,24},{24,28},{28,0},{1,5},{5... | collective-permute-start | bytes 983048 | tf_op jit(solution)/shard_map/ppermute | solution.py:33
  118.0 56.6 %collective-permute-start.22 = (bf16[128,1408]{1,0:T(8,128)(2,1)}, bf16[128,1408]{1,0:T(8,128)(2,1)}, u32[]{:S(2)}, u32[]{:S(2)}) collective-permute-start(bf16[128,1408]{1,0:T(8,128)(2,1)} %copy.162), channel_id=1, source_target_pairs={{0,4},{4,8},{8,12},{12,16},{16,20},{20,24},{24,28},{28,0},{1,5},{5... | collective-permute-start | bytes 1081352 | tf_op jit(solution)/shard_map/ppermute | solution.py:33
  120.9 47.3 %collective-permute-start.34 = (bf16[128,704]{0,1:T(8,128)(2,1)}, bf16[128,704]{0,1:T(8,128)(2,1)S(1)}, u32[]{:S(2)}, u32[]{:S(2)}) collective-permute-start(bf16[128,704]{0,1:T(8,128)(2,1)} %collective-permute-done.33), channel_id=1, source_target_pairs={{4,0},{8,4},{12,8},{16,12},{20,16},{24,20},{28,24},{0,28},{5,1},{9... | collective-permute-start | bytes 540680 | tf_op jit(solution)/shard_map/ppermute | solution.py:35
  155.3 69.5 %collective-permute-start.15 = (bf16[1024,896]{1,0:T(8,128)(2,1)}, bf16[1024,896]{1,0:T(8,128)(2,1)}, u32[]{:S(2)}, u32[]{:S(2)}) collective-permute-start(bf16[1024,896]{1,0:T(8,128)(2,1)} %bitcast.375), channel_id=1, source_target_pairs={{0,2},{2,0},{1,3},{3,1},{4,6},{6,4},{5,7},{7,5},{8,10},{10,8},{9,1... | collective-permute-start | bytes 5505032 | tf_op jit(solution)/shard_map/ppermute | solution.py:128
  162.2 136.3 %all-to-all-start.1 = ((bf16[16,32,1024]{2,1,0:T(8,128)(2,1)}), bf16[16,32,1024]{2,1,0:T(8,128)(2,1)}, u32[]{:S(2)}, u32[]{:S(2)}) async-start(bf16[16,32,1024]{2,1,0:T(8,128)(2,1)} %param.21), calls=%async_computation.1 | async-start | bytes 2097152 | tf_op jit(solution)/shard_map/all_to_all | solution.py:169
  168.2 51.7 %collective-permute-start.7 = (bf16[512,1024]{1,0:T(8,128)(2,1)}, bf16[512,1024]{1,0:T(8,128)(2,1)}, u32[]{:S(2)}, u32[]{:S(2)}) collective-permute-start(bf16[512,1024]{1,0:T(8,128)(2,1)} %fusion.52), channel_id=1, source_target_pairs={{0,1},{1,0},{2,3},{3,2},{4,5},{5,4},{6,7},{7,6},{8,9},{9,8},{10,11... | collective-permute-start | bytes 3145736 | tf_op jit(solution)/shard_map/ppermute | solution.py:64
  193.9 202.3 %collective-permute-start.35 = (bf16[128,704]{0,1:T(8,128)(2,1)}, bf16[128,704]{0,1:T(8,128)(2,1)}, u32[]{:S(2)}, u32[]{:S(2)}) collective-permute-start(bf16[128,704]{0,1:T(8,128)(2,1)} %copy-done.106), channel_id=1, source_target_pairs={{4,0},{8,4},{12,8},{16,12},{20,16},{24,20},{28,24},{0,28},{5,1},{9... | collective-permute-start | bytes 540680 | tf_op jit(solution)/shard_map/ppermute | solution.py:35
  207.3 173.3 %collective-permute-start.28 = (bf16[128,1408]{1,0:T(8,128)(2,1)}, bf16[128,1408]{1,0:T(8,128)(2,1)}, u32[]{:S(2)}, u32[]{:S(2)}) collective-permute-start(bf16[128,1408]{1,0:T(8,128)(2,1)} %collective-permute-done.27), channel_id=1, source_target_pairs={{4,0},{8,4},{12,8},{16,12},{20,16},{24,20},{28,24},{0,28},{5,1},{9... | collective-permute-start | bytes 1081352 | tf_op jit(solution)/shard_map/ppermute | solution.py:35
  210.0 72.8 %collective-permute-start.24 = (bf16[128,1408]{1,0:T(8,128)(2,1)}, bf16[128,1408]{1,0:T(8,128)(2,1)}, u32[]{:S(2)}, u32[]{:S(2)}) collective-permute-start(bf16[128,1408]{1,0:T(8,128)(2,1)} %collective-permute-done.23), channel_id=1, source_target_pairs={{0,4},{4,8},{8,12},{12,16},{16,20},{20,24},{24,28},{28,0},{1,5},{5... | collective-permute-start | bytes 1081352 | tf_op jit(solution)/shard_map/ppermute | solution.py:33
  219.9 58.6 %collective-permute-start.16 = (bf16[1024,1280]{1,0:T(8,128)(2,1)}, bf16[1024,1280]{1,0:T(8,128)(2,1)}, u32[]{:S(2)}, u32[]{:S(2)}) collective-permute-start(bf16[1024,1280]{1,0:T(8,128)(2,1)} %bitcast.339), channel_id=1, source_target_pairs={{0,2},{2,0},{1,3},{3,1},{4,6},{6,4},{5,7},{7,5},{8,10},{10,8},{9,1... | collective-permute-start | bytes 7864328 | tf_op jit(solution)/shard_map/ppermute | solution.py:128
  298.4 105.7 %all-to-all-start.3 = ((bf16[16,32,1024]{2,1,0:T(8,128)(2,1)}), bf16[16,32,1024]{2,1,0:T(8,128)(2,1)}, u32[]{:S(2)}, u32[]{:S(2)}) async-start(bf16[16,32,1024]{2,1,0:T(8,128)(2,1)} %param.22), calls=%async_computation.3 | async-start | bytes 2097152 | tf_op jit(solution)/shard_map/all_to_all | solution.py:169
  302.8 705.7 %reduce-scatter.20.cloned.1.call-start = ((), (), s32[]{:S(2)}) async-start(), calls=%async_computation.14 | async-start | bytes 1769472
  386.8 65.7 %collective-permute-start.36 = (bf16[1024,1408]{1,0:T(8,128)(2,1)}, bf16[1024,1408]{1,0:T(8,128)(2,1)}, u32[]{:S(2)}, u32[]{:S(2)}) collective-permute-start(bf16[1024,1408]{1,0:T(8,128)(2,1)} %bitcast.371), channel_id=1, source_target_pairs={{0,2},{2,0},{1,3},{3,1},{4,6},{6,4},{5,7},{7,5},{8,10},{10,8},{9,1... | collective-permute-start | bytes 8650760 | tf_op jit(solution)/shard_map/ppermute | solution.py:128
  403.8 78.6 %collective-permute-start.37 = (bf16[1024,704]{0,1:T(8,128)(2,1)}, bf16[1024,704]{0,1:T(8,128)(2,1)}, u32[]{:S(2)}, u32[]{:S(2)}) collective-permute-start(bf16[1024,704]{0,1:T(8,128)(2,1)} %copy_bitcast_fusion), channel_id=1, source_target_pairs={{0,2},{2,0},{1,3},{3,1},{4,6},{6,4},{5,7},{7,5},{8,10},{10,8},{9,1... | collective-permute-start | bytes 4325384 | tf_op jit(solution)/shard_map/ppermute | solution.py:128
  405.6 52.7 %collective-permute-start.39 = (bf16[512,1024]{1,0:T(8,128)(2,1)S(1)}, bf16[512,1024]{1,0:T(8,128)(2,1)S(1)}, u32[]{:S(2)}, u32[]{:S(2)}) collective-permute-start(bf16[512,1024]{1,0:T(8,128)(2,1)S(1)} %fusion.47), channel_id=1, source_target_pairs={{0,1},{1,0},{2,3},{3,2},{4,5},{5,4},{6,7},{7,6},{8,9},{9,8},{10,11... | collective-permute-start | bytes 3145736 | tf_op jit(solution)/shard_map/ppermute | solution.py:64
  596.4 137.7 %collective-permute-start.48 = (bf16[1024,1408]{1,0:T(8,128)(2,1)}, bf16[1024,1408]{1,0:T(8,128)(2,1)}, u32[]{:S(2)}, u32[]{:S(2)}) collective-permute-start(bf16[1024,1408]{1,0:T(8,128)(2,1)} %convolution_convert_fusion), channel_id=1, source_target_pairs={{0,2},{2,0},{1,3},{3,1},{4,6},{6,4},{5,7},{7,5},{8,10},{10,8},{9,1... | collective-permute-start | bytes 8650760 | tf_op jit(solution)/shard_map/ppermute | solution.py:132
  621.5 396.6 %reduce-scatter.22.cloned.1.call-start = ((), (), s32[]{:S(2)}) async-start(), calls=%async_computation.15 | async-start | bytes 589824
  733.6 292.0 %reduce-scatter.14.cloned.1.call-start = ((), (), s32[]{:S(2)}) async-start(), calls=%async_computation.11 | async-start | bytes 3244032 | tf_op jit(solution)/shard_map/reduce_scatter | solution.py:134
  742.3 289.7 %reduce-scatter.18.cloned.1.call-start = ((), (), s32[]{:S(2)}) async-start(), calls=%async_computation.13 | async-start | bytes 2359296
  765.2 48.0 %collective-permute-start.47 = (bf16[1024,1024]{0,1:T(8,128)(2,1)}, bf16[1024,1024]{0,1:T(8,128)(2,1)}, u32[]{:S(2)}, u32[]{:S(2)}) collective-permute-start(bf16[1024,1024]{0,1:T(8,128)(2,1)} %pad_maximum_fusion.10), channel_id=1, source_target_pairs={{0,2},{2,0},{1,3},{3,1},{4,6},{6,4},{5,7},{7,5},{8,10},{10,8},{9,1... | collective-permute-start | bytes 6291464 | tf_op jit(solution)/shard_map/ppermute | solution.py:132
  828.2 53.5 %collective-permute-start.46 = (bf16[1024,1024]{0,1:T(8,128)(2,1)}, bf16[1024,1024]{0,1:T(8,128)(2,1)}, u32[]{:S(2)}, u32[]{:S(2)}) collective-permute-start(bf16[1024,1024]{0,1:T(8,128)(2,1)} %pad_maximum_fusion.9), channel_id=1, source_target_pairs={{0,2},{2,0},{1,3},{3,1},{4,6},{6,4},{5,7},{7,5},{8,10},{10,8},{9,1... | collective-permute-start | bytes 6291464 | tf_op jit(solution)/shard_map/ppermute | solution.py:132
  836.0 50.8 %collective-permute-start.45 = (f32[512,1024]{1,0:T(8,128)}, f32[512,1024]{1,0:T(8,128)}, u32[]{:S(2)}, u32[]{:S(2)}) collective-permute-start(f32[512,1024]{1,0:T(8,128)} %slice.258), channel_id=1, source_target_pairs={{0,1},{1,0},{2,3},{3,2},{4,5},{5,4},{6,7},{7,6},{8,9},{9,8},{10,11... | collective-permute-start | bytes 6291464 | tf_op jit(solution)/shard_map/ppermute | solution.py:69
  849.1 52.3 %all-to-all-start.2 = ((bf16[16,2,16384]{2,1,0:T(2,128)(2,1)}), bf16[16,2,16384]{2,1,0:T(2,128)(2,1)}, u32[]{:S(2)}, u32[]{:S(2)}) async-start(bf16[16,2,16384]{2,1,0:T(2,128)(2,1)} %reshape.570), calls=%async_computation.2 | async-start | bytes 2097152 | tf_op jit(solution)/shard_map/all_to_all | solution.py:173
  854.8 191.6 %reduce-scatter.16.cloned.1.call-start = ((), (), s32[]{:S(2)}) async-start(), calls=%async_computation.12 | async-start | bytes 2359296
  901.5 37.5 %all-to-all-start.5 = ((bf16[16,2,16384]{2,1,0:T(2,128)(2,1)}), bf16[16,2,16384]{2,1,0:T(2,128)(2,1)}, u32[]{:S(2)}, u32[]{:S(2)}) async-start(bf16[16,2,16384]{2,1,0:T(2,128)(2,1)} %reshape.574), calls=%async_computation.5 | async-start | bytes 2097152 | tf_op jit(solution)/shard_map/all_to_all | solution.py:173
  939.0 95.1 %all-to-all-start.4 = ((bf16[16,2,16384]{2,1,0:T(2,128)(2,1)}), bf16[16,2,16384]{2,1,0:T(2,128)(2,1)S(1)}, u32[]{:S(2)}, u32[]{:S(2)}) async-start(bf16[16,2,16384]{2,1,0:T(2,128)(2,1)} %reshape.572), calls=%async_computation.4 | async-start | bytes 2097152 | tf_op jit(solution)/shard_map/all_to_all | solution.py:173
  (213 other events, 2877.6 us)
Sparse Core Ops, SparseCore 0:
  621.6 65.9 reduce-scatter.19
  733.7 62.9 reduce-scatter.21
  800.3 87.3 reduce-scatter.13
  891.1 84.5 reduce-scatter.17
  979.1 67.3 reduce-scatter.15
